TPU v7x, 256 devices: a whole 4x4x8 slice. The times are simulated.
256 devices in a mesh: row: 32 (over z, x_hi, core), col: 8 (over y, x_lo).
Axes of the slice: x: 4 (x_hi: 2, x_lo: 2; x = x_hi * 2 + x_lo), y: 4, z: 8, core: 2. Of those that a mesh axis runs over, the one named last changes fastest.
Arguments:
- s_matrix: bfloat16 [2, 16384, 32768], P(None, 'row', 'col'), may hold values from -0.046875 to 0.046875
- slab: bfloat16 [2, 32768, 384], P(None, ('col', 'row')), may hold values from -6 to 6
- beam_hkl: int32 [3, 32768], P(None, ('col', 'row')), may hold values from -24 to 24
Outputs:
- squared: bfloat16 [2, 16384, 384], P(None, 'row', 'col')
All inputs are finite; a program needn't handle non-finite values.
Results may differ from a plain program's by a relative error of at most 0.014.
Values may be sent and summed in bfloat16 or wider, within the bound.
A program may use at most 64 MiB of HBM per device.

v0:
```python
import jax
import jax.numpy as jnp
from jax import lax
from jax.sharding import PartitionSpec as P


def apply_phase(slab, beam_hkl):
    hkl_float = beam_hkl.astype(jnp.float32)
    angles = (
        0.61
        * (hkl_float[0] * hkl_float[0] + hkl_float[1] * hkl_float[1] + hkl_float[2] * hkl_float[2])
        + 0.29 * hkl_float[0]
        - 0.17 * hkl_float[1]
        + 0.43 * hkl_float[2]
    )
    cosine = jnp.cos(angles)[:, None]
    sine = jnp.sin(angles)[:, None]
    slab_real = slab[0].astype(jnp.float32)
    slab_imag = slab[1].astype(jnp.float32)
    phased_real = cosine * slab_real - sine * slab_imag
    phased_imag = cosine * slab_imag + sine * slab_real
    return jnp.stack([phased_real, phased_imag]).astype(jnp.bfloat16)


def per_device(s_matrix, slab, beam_hkl):
    phased = apply_phase(slab, beam_hkl)
    gathered = lax.all_gather(phased, "row", axis=1, tiled=True)
    s_real = s_matrix[0]
    s_imag = s_matrix[1]
    part_real = jnp.dot(s_real, gathered[0], preferred_element_type=jnp.float32) - jnp.dot(
        s_imag, gathered[1], preferred_element_type=jnp.float32
    )
    part_imag = jnp.dot(s_real, gathered[1], preferred_element_type=jnp.float32) + jnp.dot(
        s_imag, gathered[0], preferred_element_type=jnp.float32
    )
    totals = jnp.stack([part_real, part_imag])
    return lax.psum_scatter(totals.astype(jnp.bfloat16), "col", scatter_dimension=2, tiled=True)


def solution(mesh):
    placed = (P(None, "row", "col"), P(None, ("col", "row"), None), P(None, ("col", "row")))
    return jax.shard_map(
        per_device, mesh=mesh, in_specs=placed, out_specs=P(None, "row", "col"), check_vma=False
    )
```

profile of v0, /device:TPU:4, one launch (start us, length us, event | category | flops | bytes accessed | tf_op | source)
XLA Modules:
  0.0 166.7 jit_solution(7687445948443255985)
XLA Ops:
  6.5 0.0 all-gather.2.cloned.1.call-start
  6.5 0.7 convert_element_type.15
  7.2 0.1 cosine_bitcast_fusion
  7.3 1.1 fusion.31
  8.4 0.7 pad_maximum_fusion.1
  9.1 0.0 all-gather.2.cloned.1.call-update
  9.1 0.0 reduce-scatter.2.cloned.1.call-start
  9.2 95.0 %all-gather.2.cloned.1.call-done = bf16[2,4096,384]{2,1,0:T(8,128)(2,1)} async-done(((bf16[2,128,384]{2,1,0:T(8,128)(2,1)}), bf16[2,4096,384]{2,1,0:T(8,128)(2,1)}) %all-gather.2.cloned.1.call-update) | async-done | bytes 6291472 | tf_op jit(solution)/shard_map/all_gather | solution.py:27
  104.2 0.0 copy-start
  104.2 5.1 %fusion = f32[384,512]{1,0:T(8,128)S(1)} fusion(bf16[2,512,4096]{2,1,0:T(8,128)(2,1)} %param.3, bf16[2,4096,384]{2,1,0:T(8,128)(2,1)} %all-gather.2.cloned.1.call-done), kind=kOutput, calls=%fused_computation | convolution fusion | flops 1610612736 | bytes 8126464 | tf_op jit(solution)/shard_map/dot_general | solution.py:33
  109.3 0.4 copy-done
  109.7 0.0 copy-start.1
  109.7 3.9 %fusion.2 = f32[384,512]{1,0:T(8,128)S(1)} fusion(bf16[2,512,4096]{2,1,0:T(8,128)(2,1)S(1)} %copy-done, bf16[2,4096,384]{2,1,0:T(8,128)(2,1)} %all-gather.2.cloned.1.call-done), kind=kOutput, calls=%fused_computation.2 | convolution fusion | flops 1610612736 | bytes 8126464 | tf_op jit(solution)/shard_map/dot_general | solution.py:30
  113.7 0.0 copy-done.1
  113.7 1.8 %fusion.27 = bf16[1,512,384]{1,2,0:T(8,128)(2,1)S(1)} fusion(f32[384,512]{1,0:T(8,128)S(1)} %fusion, bf16[2,512,4096]{2,1,0:T(8,128)(2,1)S(1)} %copy-done, bf16[2,4096,384]{2,1,0:T(8,128)(2,1)S(1)} %copy-done.1), kind=kOutput, calls=%fused_computation.19 | convolution fusion | flops 1611005952 | bytes 8519680 | tf_op jit(solution)/shard_map/dot_general | solution.py:33
  115.5 1.8 %fusion.24 = bf16[1,512,384]{1,2,0:T(8,128)(2,1)S(1)} fusion(f32[384,512]{1,0:T(8,128)S(1)} %fusion.2, bf16[2,512,4096]{2,1,0:T(8,128)(2,1)S(1)} %copy-done, bf16[2,4096,384]{2,1,0:T(8,128)(2,1)S(1)} %copy-done.1), kind=kOutput, calls=%fused_computation.18 | convolution fusion | flops 1611005952 | bytes 8519680 | tf_op jit(solution)/shard_map/dot_general | solution.py:30
  117.4 1.0 pad_maximum_fusion
  118.3 0.0 reduce-scatter.2.cloned.1.call-update
  118.3 41.5 %reduce-scatter.2.cloned.1.call-done = bf16[2,512,48]{1,2,0:T(8,128)(2,1)} async-done(((bf16[2,512,384]{1,2,0:T(8,128)(2,1)}), bf16[2,512,48]{1,2,0:T(8,128)(2,1)}) %reduce-scatter.2.cloned.1.call-update) | async-done | bytes 98320 | tf_op jit(solution)/shard_map/reduce_scatter | solution.py:37
  (1 shorter events, 0.0 us)
Async XLA Ops:
  6.5 97.7 %all-gather.2.cloned.1.call-start = ((), (), s32[]{:S(2)}) async-start(), calls=%async_computation.1 | async-start | bytes 6488064 | tf_op jit(solution)/shard_map/all_gather | solution.py:27
  9.1 150.7 %reduce-scatter.2.cloned.1.call-start = ((), (), s32[]{:S(2)}) async-start(), calls=%async_computation.2 | async-start | bytes 884736 | tf_op jit(solution)/shard_map/reduce_scatter | solution.py:37
  104.2 5.5 %copy-start = (bf16[2,512,4096]{2,1,0:T(8,128)(2,1)S(1)}, bf16[2,512,4096]{2,1,0:T(8,128)(2,1)}, u32[]{:S(2)}) copy-start(bf16[2,512,4096]{2,1,0:T(8,128)(2,1)} %param.3) | copy-start | bytes 25165828
  109.7 3.9 %copy-start.1 = (bf16[2,4096,384]{2,1,0:T(8,128)(2,1)S(1)}, bf16[2,4096,384]{2,1,0:T(8,128)(2,1)}, u32[]{:S(2)}) copy-start(bf16[2,4096,384]{2,1,0:T(8,128)(2,1)} %all-gather.2.cloned.1.call-done) | copy-start | bytes 18874372
Sparse Core Ops, SparseCore 0:
  10.0 94.1 all-gather.1
  118.5 41.3 reduce-scatter.1
where the time goes:
time: 167 us
  waiting for transfers between devices  137 us (82%)
  between operations  13.5 us (8%)
  matrix products  12.7 us (8%)
  other arithmetic  3.46 us (2%)
    all_gather x1, waiting for transfers between devices, per_device(): gathered = lax.all_gather(phased, 'row', axis=1, tiled=True)  95 us
    reduce_scatter x1, waiting for transfers between devices, per_device(): lax.psum_scatter(totals.astype(jnp.bfloat16), 'col', scatter_dimension=2,...  41.5 us
    dot_general x1, matrix products, per_device(): jnp.dot(s_imag, gathered[0], preferred_element_type=jnp.float32)  5.11 us
    dot_general x1, matrix products, per_device(): jnp.dot(s_imag, gathered[1], preferred_element_type=jnp.float32)  3.93 us
  transfers between devices with their start and end apart: 2, of which 2 were waited for; matrix products, arithmetic and copies ran while one was open for 0% of the time, Pallas kernels for 0%

commit v1 on v0

--- a/solution.py
+++ b/solution.py
@@ -24,7 +24,8 @@
 
 def per_device(s_matrix, slab, beam_hkl):
     phased = apply_phase(slab, beam_hkl)
-    gathered = lax.all_gather(phased, "row", axis=1, tiled=True)
+    repeated = jnp.stack([phased] * lax.axis_size("row"))
+    gathered = jnp.concatenate(lax.all_to_all(repeated, "row", 0, 0), axis=1)
     s_real = s_matrix[0]
     s_imag = s_matrix[1]
     part_real = jnp.dot(s_real, gathered[0], preferred_element_type=jnp.float32) - jnp.dot(

time: 167 us -> 219 us (1.31)
  blocking collectives: 0 us -> 153 us
  waiting for transfers between devices: 137 us -> 38.7 us
  matrix products: 12.7 us -> 7.33 us
  local copies, waits for them, and re-layouts: 0.44 us -> 3.22 us
    all_to_all x0 -> x1, blocking collectives: none -> 153 us  [per_device(): gathered = jnp.concatenate(lax.all_to_all(repeated, 'row', 0, 0), axis=1)]
    all_gather x1 -> x0, waiting for transfers between devices: 95 us -> none  [per_device(): gathered = lax.all_gather(phased, 'row', axis=1, tiled=True)]
    dot_general x1, matrix products: 5.11 us -> 1.83 us  [per_device(): jnp.dot(s_imag, gathered[0], preferred_element_type=jnp.float32)]
    reduce_scatter x1, waiting for transfers between devices: 41.5 us -> 38.7 us  [per_device(): lax.psum_scatter(totals.astype(jnp.bfloat16), 'col', scatter_dimension=2,...]
  transfers between devices with their start and end apart: 2 -> 1, of which waited for: 2 -> 1; matrix products, arithmetic and copies ran while one was open for 0% -> 0% of each run, Pallas kernels for 0% -> 0%
where the time goes in v1:
time: 219 us; the launch traced here: 218 us
  blocking collectives  153 us (70%)
  waiting for transfers between devices  38.7 us (18%)
  between operations  13.5 us (6%)
  matrix products  7.33 us (3%)
  local copies, waits for them, and re-layouts  3.22 us (1%)
  other arithmetic  2.79 us (1%)
    all_to_all x1, blocking collectives, per_device(): gathered = jnp.concatenate(lax.all_to_all(repeated, 'row', 0, 0), axis=1)  153 us
    reduce_scatter x1, waiting for transfers between devices, per_device(): lax.psum_scatter(totals.astype(jnp.bfloat16), 'col', scatter_dimension=2,...  38.7 us
  transfers between devices with their start and end apart: 1, of which 1 were waited for; matrix products, arithmetic and copies ran while one was open for 0% of the time, Pallas kernels for 0%

profile of v1, /device:TPU:4, one launch (start us, length us, event | category | flops | bytes accessed | tf_op | source)
XLA Modules:
  0.0 218.4 jit_solution(11321501463978996665)
XLA Ops:
  6.5 0.0 reduce-scatter.2.cloned.1.call-start
  6.5 0.7 convert_element_type.17
  7.2 0.1 cosine_bitcast_fusion
  7.3 1.1 fusion.31
  8.4 1.0 stack.14
  9.4 0.0 slice-start
  9.5 152.9 %all_to_all.5 = bf16[32,2,128,384]{3,2,1,0:T(8,128)(2,1)S(1)} all-to-all(bf16[32,2,128,384]{3,2,1,0:T(8,128)(2,1)S(1)} %stack.14), channel_id=1, replica_groups=mesh['row'=32,'col'=8] {'row'}, dimensions={0} | all-to-all | bytes 12582912 | tf_op jit(solution)/shard_map/all_to_all | solution.py:28
  162.4 0.0 slice-start.1
  162.4 1.2 fusion.34
  163.5 0.0 slice-done
  163.5 1.0 slice-done.1
  164.6 1.8 fusion
  166.4 1.8 fusion.2
  168.2 1.8 fusion.27
  170.1 1.8 fusion.24
  171.9 1.0 pad_maximum_fusion
  172.9 0.0 reduce-scatter.2.cloned.1.call-update
  172.9 38.7 %reduce-scatter.2.cloned.1.call-done = bf16[2,512,48]{1,2,0:T(8,128)(2,1)} async-done(((bf16[2,512,384]{1,2,0:T(8,128)(2,1)}), bf16[2,512,48]{1,2,0:T(8,128)(2,1)}) %reduce-scatter.2.cloned.1.call-update) | async-done | bytes 98320 | tf_op jit(solution)/shard_map/reduce_scatter | solution.py:38
  (3 shorter events, 0.1 us)
Async XLA Ops:
  6.5 205.1 %reduce-scatter.2.cloned.1.call-start = ((), (), s32[]{:S(2)}) async-start(), calls=%async_computation.2 | async-start | bytes 884736 | tf_op jit(solution)/shard_map/reduce_scatter | solution.py:38
  9.4 154.1 %slice-start = ((s8[8388608]{0:T(1024)(128)(4,1)}), s8[4194304]{0:T(1024)(128)(4,1)S(1)}, s32[]{:S(2)}) async-start(s8[8388608]{0:T(1024)(128)(4,1)} %bitcast.46), calls=%async_computation.3 | async-start | bytes 8388608
  162.4 2.2 %slice-start.1 = ((s8[8388608]{0:T(1024)(128)(4,1)}), s8[4194304]{0:T(1024)(128)(4,1)S(1)}, s32[]{:S(2)}) async-start(s8[8388608]{0:T(1024)(128)(4,1)} %bitcast.46), calls=%async_computation.4 | async-start | bytes 8388608
Sparse Core Ops, SparseCore 0:
  173.0 38.5 reduce-scatter.1
